TPU v7x, 256 devices: a whole 4x4x8 slice. The times are simulated.
256 devices in a mesh: sens: 64 (over z_hi, y, x, core), hour: 4 (over z_lo).
Axes of the slice: x: 4, y: 4, z: 8 (z_hi: 2, z_lo: 4; z = z_hi * 4 + z_lo), core: 2. Of those that a mesh axis runs over, the one named last changes fastest.
Arguments:
- sky: bfloat16 [512, 146], P('hour'), may hold values from 0.049804688 to 1
- sky_open: bfloat16 [146, 131072], P(None, 'sens'), may hold values from 0 to 0.013977051
- sky_closed: bfloat16 [146, 131072], P(None, 'sens'), may hold values from 0 to 0.0039978027
- sun_coef: bfloat16 [5165, 131072], P(None, ('sens', 'hour')), may hold values from 0 to 1
- sun_bins: int32 [512, 4], P('hour'), may hold values from 0 to 5164, as said below
- sun_rad: bfloat16 [512, 4], P('hour'), may hold values from 0.099609375 to 1
- target: bfloat16 [512, 131072], P('hour', 'sens'), may hold values from 0 to 2
- zone_of: int32 [65536, 1], P('sens'), may hold values from 0 to 63
- area: float32 [65536], P('sens'), may hold values from 0.5 to 4
- openness: float32 [65536], P('sens'), may hold values from 0 to 1
Outputs:
- illuminance: bfloat16 [512, 131072], P('hour', 'sens')
- new_openness: float32 [65536], P('sens')
Inputs may be any that keep to these rules, and one draw needn't show every extreme that they name: `sun_bins`: the 4 bins of one hour are consecutive modulo 5165, hence distinct. `zone_of`: every zone has at least one window.
All inputs are finite; a program needn't handle non-finite values.
Results may differ from a plain program's by a relative error of at most 0.001.
Values may be sent and summed in bfloat16 or wider, within the bound.
A program may use at most 128 MiB of HBM per device.

v0:
```python
import jax
import jax.numpy as jnp
from jax import lax
from jax.sharding import PartitionSpec as P


def local(sky, sky_open, sky_closed, sun_coef, sun_bins, sun_rad, target, zone_of, area, openness):
    zone_count = lax.axis_size("sens")
    own_zone = lax.axis_index("sens")
    member = (zone_of[:, 0][:, None] == jnp.arange(zone_count, dtype=jnp.int32)[None, :]).astype(
        jnp.float32
    )
    stacked = jnp.stack([area * openness, area])
    partial_sums = jnp.dot(stacked, member, precision=lax.Precision.HIGHEST)
    totals = lax.psum(partial_sums, "sens")
    mine = lax.dynamic_slice_in_dim(totals, own_zone, 1, 1)[:, 0]
    share = mine[0] / mine[1]
    op_part = jnp.dot(sky, sky_open, preferred_element_type=jnp.float32)
    cl_part = jnp.dot(sky, sky_closed, preferred_element_type=jnp.float32)
    hour_rows = sky.shape[0]
    kbins = sun_bins.shape[1]
    nbins = sun_coef.shape[0]
    columns = jnp.arange(nbins, dtype=jnp.int32)[None, :]
    weights = jnp.zeros((hour_rows, nbins), jnp.float32)
    for slot in range(kbins):
        weights = weights + jnp.where(
            sun_bins[:, slot][:, None] == columns,
            sun_rad[:, slot][:, None].astype(jnp.float32),
            0.0,
        )
    weights = weights.astype(jnp.bfloat16)
    sun_part = jnp.dot(
        weights,
        lax.all_gather(sun_coef, "hour", axis=1, tiled=True),
        preferred_element_type=jnp.float32,
    )
    cross = op_part - cl_part + sun_part
    lit = cl_part + share * cross
    local_grad = jnp.sum(2.0 * (lit - target.astype(jnp.float32)) * cross)
    zone_grad = lax.psum(local_grad, "hour")
    ratio = zone_grad / mine[1]
    windows_all = area.shape[0] * zone_count
    ratio_all = lax.all_gather(ratio[None], "sens", axis=0, tiled=True)
    grad = area * jnp.dot(member, ratio_all, precision=lax.Precision.HIGHEST)
    square_sum = lax.psum(jnp.sum(grad * grad), "sens")
    rms = jnp.sqrt(square_sum / windows_all + 1e-06)
    new_openness = jnp.clip(openness - 0.25 * grad / rms, 0.0, 1.0)
    return (lit.astype(jnp.bfloat16), new_openness)


def solution(mesh):
    in_specs = (
        P("hour", None),
        P(None, "sens"),
        P(None, "sens"),
        P(None, ("sens", "hour")),
        P("hour", None),
        P("hour", None),
        P("hour", "sens"),
        P("sens", None),
        P("sens"),
        P("sens"),
    )
    out_specs = (P("hour", "sens"), P("sens"))
    return jax.shard_map(local, mesh=mesh, in_specs=in_specs, out_specs=out_specs, check_vma=False)
```

profile of v0, /device:TPU:1, one launch (start us, length us, event | category | flops | bytes accessed | tf_op | source)
XLA Modules:
  0.0 979.7 jit_solution(9576175266533174772)
XLA Ops:
  7.2 0.0 copy-start
  7.2 0.0 copy-start.9
  7.2 0.0 copy-start.4
  7.2 0.0 copy-start.5
  7.2 0.0 copy-start.8
  7.2 0.0 copy-start.6
  7.2 0.0 copy-start.7
  7.2 0.0 copy-start.3
  7.3 0.0 copy-start.1
  7.3 0.0 all-gather.2.cloned.1.call-start
  7.3 0.7 all-gather.2.cloned.1.call-update
  8.0 0.0 copy-done.4
  8.0 0.0 copy-done.5
  8.0 0.0 copy-done.8
  8.0 0.7 fusion.13
  8.8 409.5 %psum.21 = f32[2,64]{0,1:T(8,128)S(1)} all-reduce(f32[2,64]{0,1:T(8,128)S(1)} %fusion.13), channel_id=1, replica_groups=mesh['sens'=64,'hour'=4] {'sens'}, use_global_device_ids=true, to_apply=%region_0.0 | all-reduce | flops 128 | bytes 1024 | tf_op jit(solution)/shard_map/psum | solution.py:15
  418.3 0.6 fusion.22
  420.2 0.0 copy-done.9
  420.2 0.7 dynamic-slice
  420.9 0.0 copy-done.6
  420.9 0.0 copy-done.7
  420.9 0.0 copy-done.3
  420.9 0.0 copy-done.1
  420.9 0.3 fusion.23
  421.3 0.0 all-gather.2.cloned.1.call-done
  421.3 0.0 copy-start.2
  421.3 11.0 %fusion.1 = f32[128,2048]{1,0:T(8,128)S(1)} fusion(bf16[5165,2048]{1,0:T(8,128)(2,1)} %all-gather.2.cloned.1.call-done, f32[128]{0:T(128)S(1)} %get-tuple-element.10, s32[128]{0:T(128)S(1)} %get-tuple-element.6, f32[128]{0:T(128)S(1)} %get-tuple-element.11, s32[128]{0:T(128)S(1)} %get-tuple-element.7, f32[128]{0:T(128)S(1)} %get-tuple-element.9, ...), kind=kOutput, calls=%fused_computation.7 | convolution fusion | flops 2715880960 | bytes 22208512 | tf_op jit(solution)/shard_map/dot_general | solution.py:32
  432.3 0.0 copy-done
  432.3 0.0 copy-done.2
  432.4 2.0 multiply_reduce_fusion
  434.4 119.7 %psum.22 = f32[]{:T(128)} all-reduce(f32[]{:T(128)} %get-tuple-element.2), channel_id=1, replica_groups=mesh['sens'=64,'hour'=4] {'hour'}, use_global_device_ids=true, to_apply=%region_2.3 | all-reduce | flops 1 | bytes 8 | tf_op jit(solution)/shard_map/psum | solution.py:40
  555.4 0.8 dynamic-update-slice
  556.2 212.8 %all-reduce = f32[64]{0:T(128)S(1)} all-reduce(f32[64]{0:T(128)S(1)} %dynamic-update-slice), channel_id=1, replica_groups=mesh['sens'=64,'hour'=4] {'sens'}, use_global_device_ids=true, to_apply=%add | all-reduce | flops 64 | bytes 512
  768.9 0.4 fusion.12
  769.4 0.6 multiply_reduce_fusion.1
  770.0 201.6 %psum.23 = f32[]{:T(128)} all-reduce(f32[]{:T(128)} %multiply_reduce_fusion.1), channel_id=1, replica_groups=mesh['sens'=64,'hour'=4] {'sens'}, use_global_device_ids=true, to_apply=%region_4.5 | all-reduce | flops 1 | bytes 8 | tf_op jit(solution)/shard_map/psum | solution.py:45
  972.3 0.6 subtract_clamp_fusion
  (5 shorter events, 0.0 us)
Async XLA Ops:
  7.2 425.2 %copy-start = (bf16[146,2048]{1,0:T(8,128)(2,1)S(1)}, bf16[146,2048]{1,0:T(8,128)(2,1)}, u32[]{:S(2)}) copy-start(bf16[146,2048]{1,0:T(8,128)(2,1)} %param.11) | copy-start | bytes 1794052
  7.2 413.0 %copy-start.9 = (u32[256]{0:T(256)S(1)}, u32[256]{0:T(256)}, u32[]{:S(2)}) copy-start(u32[256]{0:T(256)} %constant.25) | copy-start | bytes 3076
  7.2 0.8 copy-start.4
  7.2 0.8 copy-start.5
  7.2 0.8 copy-start.8
  7.2 413.7 %copy-start.6 = (bf16[128,4]{0,1:T(4,128)(2,1)S(1)}, bf16[128,4]{0,1:T(4,128)(2,1)}, u32[]{:S(2)}) copy-start(bf16[128,4]{0,1:T(4,128)(2,1)} %param.15) | copy-start | bytes 3076
  7.2 413.7 %copy-start.7 = (s32[128,4]{0,1:T(4,128)S(1)}, s32[128,4]{0,1:T(4,128)}, u32[]{:S(2)}) copy-start(s32[128,4]{0,1:T(4,128)} %param.14) | copy-start | bytes 6148
  7.2 413.7 %copy-start.3 = (bf16[128,146]{0,1:T(8,128)(2,1)S(1)}, bf16[128,146]{0,1:T(8,128)(2,1)}, u32[]{:S(2)}) copy-start(bf16[128,146]{0,1:T(8,128)(2,1)} %param.10) | copy-start | bytes 112132
  7.3 413.7 %copy-start.1 = (bf16[146,2048]{1,0:T(8,128)(2,1)S(1)}, bf16[146,2048]{1,0:T(8,128)(2,1)}, u32[]{:S(2)}) copy-start(bf16[146,2048]{1,0:T(8,128)(2,1)} %param.12) | copy-start | bytes 1794052
  7.3 414.0 %all-gather.2.cloned.1.call-start = ((), (), s32[]{:S(2)}) async-start(), calls=%async_computation | async-start | bytes 26460160 | tf_op jit(solution)/shard_map/all_gather | solution.py:34
  421.3 11.0 %copy-start.2 = (bf16[128,2048]{1,0:T(8,128)(2,1)S(1)}, bf16[128,2048]{1,0:T(8,128)(2,1)}, u32[]{:S(2)}) copy-start(bf16[128,2048]{1,0:T(8,128)(2,1)} %param.16) | copy-start | bytes 1572868
Sparse Core Ops, SparseCore 0:
  9.9 370.8 all-gather.1
where the time goes:
time: 980 us
  blocking collectives  944 us (96%)
  between operations  17.5 us (2%)
  matrix products  14.5 us (1%)
    psum x1, blocking collectives, local(): totals = lax.psum(partial_sums, 'sens')  409 us
    unnamed x1, blocking collectives  213 us
    psum x1, blocking collectives, local(): square_sum = lax.psum(jnp.sum(grad * grad), 'sens')  202 us
    psum x1, blocking collectives, local(): zone_grad = lax.psum(local_grad, 'hour')  120 us
  transfers between devices with their start and end apart: 1, of which 0 were waited for; matrix products, arithmetic and copies ran while one was open for 0% of the time, Pallas kernels for 0%

commit v1 on v0

v1 whole, which is shorter than its diff:
```python
import functools

import jax
import jax.numpy as jnp
from jax import lax
from jax.experimental import pallas as pl
from jax.experimental.pallas import tpu as pltpu
from jax.sharding import PartitionSpec as P

MESH = pl.DeviceIdType.MESH
F32 = jnp.float32
BF16 = jnp.bfloat16
HIGH = lax.Precision.HIGHEST
SIDE = 8
LANES = 128
ROWS = 32


def kernel(
    hours,
    windows_all,
    sky_hbm,
    open_hbm,
    closed_hbm,
    coef_hbm,
    bins_ref,
    rad_ref,
    target_hbm,
    zone_ref,
    area_ref,
    openness_ref,
    lit_hbm,
    new_ref,
    coef,
    tail_wide,
    tail,
    weights,
    columns,
    bins,
    sky,
    target,
    open_own,
    closed_own,
    cross,
    lit,
    lit_out,
    member,
    stat_a,
    stat_b,
    grad_h,
    grad_a,
    grad_b,
    local_sem,
    hour_send,
    hour_recv,
    side_send,
    side_recv,
):
    s = lax.axis_index("sens")
    h = lax.axis_index("hour")
    low = lax.rem(s, SIDE)
    high = s // SIDE
    nbins, own = coef.shape
    block = sky.shape[2]
    whole = nbins // LANES * LANES
    zones = zone_ref.shape[1] * 0 + SIDE * SIDE

    def hour_of(d):
        return (s, lax.rem(h + d, hours))

    def back_of(d):
        return (s, lax.rem(h + hours - d, hours))

    def low_of(d):
        return (high * SIDE + lax.rem(low + d, SIDE), h)

    def high_of(d):
        return (lax.rem(high + d, SIDE) * SIDE + low, h)

    barrier = pltpu.get_barrier_semaphore()
    for d in range(1, hours):
        pl.semaphore_signal(barrier, inc=1, device_id=hour_of(d), device_id_type=MESH)
    for d in range(1, SIDE):
        pl.semaphore_signal(barrier, inc=1, device_id=low_of(d), device_id_type=MESH)
        pl.semaphore_signal(barrier, inc=1, device_id=high_of(d), device_id_type=MESH)

    own_columns = pl.ds(pl.multiple_of(h * own, own), own)
    chunk = 1024
    local = []
    for at in range(0, nbins, chunk):
        rows = pl.ds(at, min(chunk, nbins - at))
        local.append(pltpu.make_async_copy(coef_hbm.at[rows], coef.at[rows], local_sem.at[len(local)]))
    local.append(pltpu.make_async_copy(open_hbm.at[:, own_columns], open_own, local_sem.at[len(local)]))
    local.append(pltpu.make_async_copy(closed_hbm.at[:, own_columns], closed_own, local_sem.at[len(local)]))
    local.append(pltpu.make_async_copy(target_hbm.at[:, own_columns], target.at[0], local_sem.at[len(local)]))
    sky_copy = pltpu.make_async_copy(sky_hbm, sky.at[0], local_sem.at[len(local)])
    local.append(sky_copy)
    for copy in local:
        copy.start()

    bins[0, 0:4, :] = bins_ref[...].astype(F32)
    bins[0, 4:8, :] = rad_ref[...].astype(F32)

    area = area_ref[...]
    row = lax.broadcasted_iota(jnp.int32, (SIDE, area.shape[1]), 0)
    zone_row = lax.broadcasted_iota(jnp.int32, member.shape, 0)
    member[...] = jnp.where(zone_row == zone_ref[...], 1.0, 0.0).astype(F32)
    stacked = jnp.where(
        row == 0, area * openness_ref[...], jnp.where(row == 1, area, jnp.where(row == 2, area * area, 0.0))
    )
    stat_a[0] = lax.dot_general(
        stacked, member[...], (((1,), (1,)), ((), ())), precision=HIGH, preferred_element_type=F32
    )

    pl.semaphore_wait(barrier, hours - 1 + 2 * (SIDE - 1))

    def to_hour(source, target_of, d, kind, device):
        return pltpu.make_async_remote_copy(
            src_ref=source,
            dst_ref=target_of,
            send_sem=hour_send.at[kind, d],
            recv_sem=hour_recv.at[kind, d],
            device_id=device,
            device_id_type=MESH,
        )

    def to_side(buffer, d, kind, device):
        return pltpu.make_async_remote_copy(
            src_ref=buffer.at[0],
            dst_ref=buffer.at[d],
            send_sem=side_send.at[kind, d],
            recv_sem=side_recv.at[kind, d],
            device_id=device,
            device_id_type=MESH,
        )

    bins_copies = [to_hour(bins.at[0], bins.at[d], d, 0, hour_of(d)) for d in range(1, hours)]
    for copy in bins_copies:
        copy.start()
    stat_a_copies = [to_side(stat_a, d, 0, low_of(d)) for d in range(1, SIDE)]
    for copy in stat_a_copies:
        copy.start()
    sky_copies = [to_hour(sky_hbm, sky.at[d], d, 1, hour_of(d)) for d in range(1, hours)]
    for copy in sky_copies:
        copy.start()
    target_copies = []
    for d in range(1, hours):
        there = lax.rem(h + d, hours)
        place = pl.ds(pl.multiple_of(there * own, own), own)
        target_copies.append(to_hour(target_hbm.at[:, place], target.at[d], d, 2, hour_of(d)))
    for copy in target_copies:
        copy.start()

    lane = lax.broadcasted_iota(jnp.int32, (ROWS, LANES), 1).astype(F32)

    def build(d):
        columns[d * block : (d + 1) * block, :] = bins[d].T

        def rows_of(r, carry):
            at = pl.multiple_of(d * block + r * ROWS, ROWS)
            mine = columns[pl.ds(at, ROWS), :]
            place = [jnp.broadcast_to(mine[:, k : k + 1], (ROWS, LANES)) - lane for k in range(4)]
            value = [jnp.broadcast_to(mine[:, 4 + k : 5 + k], (ROWS, LANES)) for k in range(4)]
            for c in range(weights.shape[1] // LANES):
                first = float(c * LANES)
                w = jnp.zeros((ROWS, LANES), F32)
                for k in range(4):
                    w = jnp.where(place[k] == first, value[k], w)
                weights[pl.ds(at, ROWS), c * LANES : (c + 1) * LANES] = w.astype(BF16)
            return carry

        lax.fori_loop(0, block // ROWS, rows_of, 0)

    build(0)

    def total_of(buffer, me, count):
        total = buffer[lax.rem(me, count)]
        for m in range(1, count):
            total = total + buffer[lax.rem(me + count - m, count)]
        return total

    for copy in stat_a_copies:
        copy.wait_recv()
    stat_b[0] = total_of(stat_a, low, SIDE)
    stat_b_copies = [to_side(stat_b, d, 1, high_of(d)) for d in range(1, SIDE)]
    for copy in stat_b_copies:
        copy.start()

    for d in range(1, hours):
        bins_copies[d - 1].wait_recv()
        build(d)
    for copy in local:
        copy.wait()

    tail_wide[...] = jnp.zeros_like(tail_wide)
    tail_wide[0 : nbins - whole, :] = coef[whole:nbins, :].astype(F32)
    tail[...] = tail_wide[...].astype(BF16)

    for copy in stat_b_copies:
        copy.wait_recv()
    sums = total_of(stat_b, high, SIDE)
    zone_lane = lax.broadcasted_iota(jnp.int32, (1, LANES), 1)
    den = jnp.where(zone_lane < zones, sums[1:2], 1.0)
    shares = sums[0:1] / den
    share = jnp.sum(jnp.where(zone_lane == s, shares, 0.0), axis=1, keepdims=True)

    lit_copies = []
    for d in (1, 2, 3, 0):
        if d:
            sky_copies[d - 1].wait_recv()
        here = pl.ds(d * block, block)
        first = (((0,), (0,)), ((), ()))
        op_part = lax.dot_general(sky[d], open_own[...], first, preferred_element_type=F32)
        cl_part = lax.dot_general(sky[d], closed_own[...], first, preferred_element_type=F32)
        sun = jnp.dot(weights[here, 0:whole], coef[0:whole, :], preferred_element_type=F32)
        sun = sun + jnp.dot(weights[here, whole:], tail[...], preferred_element_type=F32)
        both = op_part - cl_part + sun
        cross[d] = both
        level = cl_part + share * both
        lit[d] = level
        lit_out[d] = level.astype(BF16)
        if d:
            copy = to_hour(lit_out.at[d], lit_hbm.at[:, own_columns], d, 3, back_of(d))
            copy.start()
            lit_copies.append(copy)
    own_out = pltpu.make_async_copy(lit_out.at[0], lit_hbm.at[:, own_columns], local_sem.at[0])
    own_out.start()

    terms = jnp.zeros((1, own), F32)
    for d in range(hours):
        if d:
            target_copies[d - 1].wait_recv()
        part = 2.0 * (lit[d] - target[d].astype(F32)) * cross[d]
        terms = terms + jnp.sum(part, axis=0, keepdims=True)
    local_grad = jnp.sum(terms, axis=1, keepdims=True)
    tile_lane = lax.broadcasted_iota(jnp.int32, (SIDE, LANES), 1)
    grad_h[0] = jnp.where(tile_lane == s, local_grad, 0.0)
    copies_h = [to_hour(grad_h.at[0], grad_h.at[d], d, 4, hour_of(d)) for d in range(1, hours)]
    for copy in copies_h:
        copy.start()
    for copy in copies_h:
        copy.wait_recv()
    grad_a[0] = total_of(grad_h, h, hours)
    copies_a = [to_side(grad_a, d, 2, low_of(d)) for d in range(1, SIDE)]
    for copy in copies_a:
        copy.start()
    for copy in copies_a:
        copy.wait_recv()
    grad_b[0] = total_of(grad_a, low, SIDE)
    copies_b = [to_side(grad_b, d, 3, high_of(d)) for d in range(1, SIDE)]
    for copy in copies_b:
        copy.start()
    for copy in copies_b:
        copy.wait_recv()
    zone_grad = total_of(grad_b, high, SIDE)
    ratio = zone_grad / den
    square = jnp.sum(ratio[0:1] * ratio[0:1] * sums[2:3], axis=1, keepdims=True)
    rms = jnp.sqrt(square / windows_all + 1e-06)
    spread = jnp.dot(ratio, member[...], precision=HIGH, preferred_element_type=F32)
    grad = area * spread[0:1]
    new_ref[...] = jnp.clip(openness_ref[...] - 0.25 * grad / rms, 0.0, 1.0)

    for copy in bins_copies + sky_copies + target_copies + copies_h:
        copy.wait_send()
    for copy in stat_a_copies + stat_b_copies + copies_a + copies_b:
        copy.wait_send()
    own_out.wait()
    for copy in lit_copies:
        copy.wait()


def solution(mesh):
    hours = mesh.shape["hour"]
    sens = mesh.shape["sens"]

    def step(sky, sky_open, sky_closed, sun_coef, sun_bins, sun_rad, target, zone_of, area, openness):
        block, patches = sky.shape
        nbins, own = sun_coef.shape
        windows = area.shape[0]
        padded = pl.cdiv(nbins, LANES) * LANES
        any_space = pl.BlockSpec(memory_space=pl.ANY)
        vmem = pl.BlockSpec(memory_space=pltpu.VMEM)
        tile = (SIDE, LANES)
        lit, new = pl.pallas_call(
            functools.partial(kernel, hours, windows * sens),
            out_shape=(
                jax.ShapeDtypeStruct((block, own * hours), BF16),
                jax.ShapeDtypeStruct((1, windows), F32),
            ),
            in_specs=[any_space, any_space, any_space, any_space, vmem, vmem, any_space, vmem, vmem, vmem],
            out_specs=(any_space, vmem),
            scratch_shapes=[
                pltpu.VMEM((nbins, own), BF16),
                pltpu.VMEM((LANES, own), F32),
                pltpu.VMEM((LANES, own), BF16),
                pltpu.VMEM((hours * block, padded), BF16),
                pltpu.VMEM((hours * block, SIDE), F32),
                pltpu.VMEM((hours,) + tile, F32),
                pltpu.VMEM((hours, patches, block), BF16),
                pltpu.VMEM((hours, block, own), BF16),
                pltpu.VMEM((patches, own), BF16),
                pltpu.VMEM((patches, own), BF16),
                pltpu.VMEM((hours, block, own), F32),
                pltpu.VMEM((hours, block, own), F32),
                pltpu.VMEM((hours, block, own), BF16),
                pltpu.VMEM((LANES, windows), F32),
                pltpu.VMEM((SIDE,) + tile, F32),
                pltpu.VMEM((SIDE,) + tile, F32),
                pltpu.VMEM((hours,) + tile, F32),
                pltpu.VMEM((SIDE,) + tile, F32),
                pltpu.VMEM((SIDE,) + tile, F32),
                pltpu.SemaphoreType.DMA((16,)),
                pltpu.SemaphoreType.DMA((5, hours)),
                pltpu.SemaphoreType.DMA((5, hours)),
                pltpu.SemaphoreType.DMA((4, SIDE)),
                pltpu.SemaphoreType.DMA((4, SIDE)),
            ],
            compiler_params=pltpu.CompilerParams(
                collective_id=0, has_side_effects=True, vmem_limit_bytes=48 << 20
            ),
        )(
            sky.T,
            sky_open,
            sky_closed,
            sun_coef,
            sun_bins.T,
            sun_rad.T,
            target,
            zone_of.T,
            area[None, :],
            openness[None, :],
        )
        return lit, new[0]

    in_specs = (
        P("hour", None),
        P(None, "sens"),
        P(None, "sens"),
        P(None, ("sens", "hour")),
        P("hour", None),
        P("hour", None),
        P("hour", "sens"),
        P("sens", None),
        P("sens"),
        P("sens"),
    )
    out_specs = (P("hour", "sens"), P("sens"))
    return jax.shard_map(step, mesh=mesh, in_specs=in_specs, out_specs=out_specs, check_vma=False)
```

time: 980 us -> 60.7 us (0.06)
  blocking collectives: 944 us -> 0 us
  Pallas kernels: 0 us -> 50.9 us
  between operations: 17.5 us -> 0.66 us
  matrix products: 14.5 us -> 0 us
    psum x3 -> x0, blocking collectives: 731 us -> none  [the longest x1 409 us: local(): totals = lax.psum(partial_sums, 'sens')]
    unnamed x1 -> x0, blocking collectives: 213 us -> none
    pallas_call x0 -> x1, Pallas kernels: none -> 50.9 us  [step(): pl.pallas_call(functools.partial(kernel, hours, windows * sens), out_shap...]
    dot_general x5 -> x0, matrix products: 14.5 us -> none  [the longest x1 11 us: local(): jnp.dot(weights, lax.all_gather(sun_coef, 'hour', axis=1, tiled=True), pr...]
  transfers between devices with their start and end apart: 1 -> 0, of which waited for: 0 -> 0; matrix products, arithmetic and copies ran while one was open for 0% -> 0% of each run, Pallas kernels for 0% -> 0%
where the time goes in v1:
time: 60.7 us; the launch traced here: 60.3 us
  Pallas kernels  50.9 us (84%)
  local copies, waits for them, and re-layouts  8.77 us (14%)
  between operations  0.66 us (1%)
    pallas_call x1, Pallas kernels, step(): pl.pallas_call(functools.partial(kernel, hours, windows * sens), out_shap...  50.9 us
    unnamed x20, local copies, waits for them, and re-layouts  8.77 us

profile of v1, /device:TPU:1, one launch (start us, length us, event | category | flops | bytes accessed | tf_op | source)
XLA Modules:
  0.0 60.3 jit_solution(13361944725380668952)
XLA Ops:
  0.6 0.0 copy-start
  0.6 1.1 %copy-done = bf16[146,2048]{1,0:T(8,128)(2,1)S(1)} copy-done((bf16[146,2048]{1,0:T(8,128)(2,1)S(1)}, bf16[146,2048]{1,0:T(8,128)(2,1)}, u32[]{:S(2)}) %copy-start) | copy-done | bytes 598040
  1.7 0.0 copy-start.1
  1.7 1.1 %copy-done.1 = bf16[146,2048]{1,0:T(8,128)(2,1)S(1)} copy-done((bf16[146,2048]{1,0:T(8,128)(2,1)S(1)}, bf16[146,2048]{1,0:T(8,128)(2,1)}, u32[]{:S(2)}) %copy-start.1) | copy-done | bytes 598040
  2.8 0.0 copy-start.2
  2.8 1.0 %copy-done.2 = bf16[128,2048]{1,0:T(8,128)(2,1)S(1)} copy-done((bf16[128,2048]{1,0:T(8,128)(2,1)S(1)}, bf16[128,2048]{1,0:T(8,128)(2,1)}, u32[]{:S(2)}) %copy-start.2) | copy-done | bytes 524312
  3.8 0.0 copy-start.3
  3.8 0.8 %copy-done.3 = bf16[128,146]{0,1:T(8,128)(2,1)S(1)} copy-done((bf16[128,146]{0,1:T(8,128)(2,1)S(1)}, bf16[128,146]{0,1:T(8,128)(2,1)}, u32[]{:S(2)}) %copy-start.3) | copy-done | bytes 37400
  4.6 0.0 copy-start.4
  4.6 0.7 %copy-done.4 = s32[1024,1]{0,1:T(1,128)S(1)} copy-done((s32[1024,1]{0,1:T(1,128)S(1)}, s32[1024,1]{0,1:T(1,128)}, u32[]{:S(2)}) %copy-start.4) | copy-done | bytes 4120
  5.3 0.0 copy-start.5
  5.3 0.7 %copy-done.5 = f32[1024]{0:T(1024)S(1)} copy-done((f32[1024]{0:T(1024)S(1)}, f32[1024]{0:T(1024)}, u32[]{:S(2)}) %copy-start.5) | copy-done | bytes 4120
  6.0 0.0 copy-start.6
  6.0 0.7 %copy-done.6 = f32[1024]{0:T(1024)S(1)} copy-done((f32[1024]{0:T(1024)S(1)}, f32[1024]{0:T(1024)}, u32[]{:S(2)}) %copy-start.6) | copy-done | bytes 4120
  6.7 0.0 copy-start.7
  6.7 0.7 %copy-done.7 = s32[128,4]{0,1:T(4,128)S(1)} copy-done((s32[128,4]{0,1:T(4,128)S(1)}, s32[128,4]{0,1:T(4,128)}, u32[]{:S(2)}) %copy-start.7) | copy-done | bytes 2072
  7.3 0.0 copy-start.8
  7.3 0.7 %copy-done.8 = bf16[128,4]{0,1:T(4,128)(2,1)S(1)} copy-done((bf16[128,4]{0,1:T(4,128)(2,1)S(1)}, bf16[128,4]{0,1:T(4,128)(2,1)}, u32[]{:S(2)}) %copy-start.8) | copy-done | bytes 1048
  8.0 50.9 %shard_map.113 = (bf16[128,2048]{1,0:T(8,128)(2,1)S(1)}, f32[1,1024]{1,0:T(1,128)S(1)}) custom-call(bf16[146,128]{1,0:T(8,128)(2,1)S(1)} %bitcast.7, bf16[146,2048]{1,0:T(8,128)(2,1)S(1)} %copy-done, bf16[146,2048]{1,0:T(8,128)(2,1)S(1)} %copy-done.1, bf16[5165,512]{1,0:T(8,128)(2,1)} %coef_hbm.1, s32[4,128]{1,0:T(4,128)S(1)} %bitcast.12, ...), custom_call_target="tpu_custom_call" | custom-call | tf_op jit(solution)/shard_map/pallas_call | solution.py:284
  58.9 0.8 %copy.14 = bf16[128,2048]{1,0:T(8,128)(2,1)} copy(bf16[128,2048]{1,0:T(8,128)(2,1)S(1)} %get-tuple-element.8) | data formatting | bytes 1048576
  59.7 0.6 copy.15
Async XLA Ops:
  0.6 1.1 %copy-start = (bf16[146,2048]{1,0:T(8,128)(2,1)S(1)}, bf16[146,2048]{1,0:T(8,128)(2,1)}, u32[]{:S(2)}) copy-start(bf16[146,2048]{1,0:T(8,128)(2,1)} %open_hbm.1) | copy-start | bytes 1794052
  1.7 1.1 %copy-start.1 = (bf16[146,2048]{1,0:T(8,128)(2,1)S(1)}, bf16[146,2048]{1,0:T(8,128)(2,1)}, u32[]{:S(2)}) copy-start(bf16[146,2048]{1,0:T(8,128)(2,1)} %closed_hbm.1) | copy-start | bytes 1794052
  2.8 1.0 %copy-start.2 = (bf16[128,2048]{1,0:T(8,128)(2,1)S(1)}, bf16[128,2048]{1,0:T(8,128)(2,1)}, u32[]{:S(2)}) copy-start(bf16[128,2048]{1,0:T(8,128)(2,1)} %target_hbm.1) | copy-start | bytes 1572868
  3.8 0.8 %copy-start.3 = (bf16[128,146]{0,1:T(8,128)(2,1)S(1)}, bf16[128,146]{0,1:T(8,128)(2,1)}, u32[]{:S(2)}) copy-start(bf16[128,146]{0,1:T(8,128)(2,1)} %param.10) | copy-start | bytes 112132
  4.6 0.7 %copy-start.4 = (s32[1024,1]{0,1:T(1,128)S(1)}, s32[1024,1]{0,1:T(1,128)}, u32[]{:S(2)}) copy-start(s32[1024,1]{0,1:T(1,128)} %param.17) | copy-start | bytes 12292
  5.3 0.7 %copy-start.5 = (f32[1024]{0:T(1024)S(1)}, f32[1024]{0:T(1024)}, u32[]{:S(2)}) copy-start(f32[1024]{0:T(1024)} %param.18) | copy-start | bytes 12292
  6.0 0.7 %copy-start.6 = (f32[1024]{0:T(1024)S(1)}, f32[1024]{0:T(1024)}, u32[]{:S(2)}) copy-start(f32[1024]{0:T(1024)} %param.19) | copy-start | bytes 12292
  6.7 0.7 %copy-start.7 = (s32[128,4]{0,1:T(4,128)S(1)}, s32[128,4]{0,1:T(4,128)}, u32[]{:S(2)}) copy-start(s32[128,4]{0,1:T(4,128)} %param.14) | copy-start | bytes 6148
  7.3 0.7 %copy-start.8 = (bf16[128,4]{0,1:T(4,128)(2,1)S(1)}, bf16[128,4]{0,1:T(4,128)(2,1)}, u32[]{:S(2)}) copy-start(bf16[128,4]{0,1:T(4,128)(2,1)} %param.15) | copy-start | bytes 3076

commit v2 on v1

v2 whole, which is shorter than its diff:
```python
import functools

import jax
import jax.numpy as jnp
from jax import lax
from jax.experimental import pallas as pl
from jax.experimental.pallas import tpu as pltpu
from jax.sharding import PartitionSpec as P

MESH = pl.DeviceIdType.MESH
F32 = jnp.float32
BF16 = jnp.bfloat16
HIGH = lax.Precision.HIGHEST
SIDE = 8
YS = 4
PLANE = SIDE * YS
PIECE = 24
LANES = 128
ROWS = 32


def kernel(
    hours,
    windows_all,
    sky_hbm,
    open_hbm,
    closed_hbm,
    coef_hbm,
    bins_hbm,
    rad_hbm,
    target_hbm,
    zone_hbm,
    area_hbm,
    openness_hbm,
    lit_hbm,
    new_ref,
    bins_ref,
    rad_ref,
    zone_ref,
    area_ref,
    openness_ref,
    coef,
    tail_wide,
    tail,
    weights,
    columns,
    bins,
    sky_in,
    sky,
    target,
    open_own,
    closed_own,
    cross,
    lit,
    lit_out,
    member,
    stat_low,
    stat_y,
    stat_half,
    grad_z,
    grad_plane,
    local_sem,
    hour_send,
    hour_recv,
    low_send,
    low_recv,
    y_send,
    y_recv,
    half_send,
    half_recv,
    z_send,
    z_recv,
    plane_send,
    plane_recv,
):
    s = lax.axis_index("sens")
    h = lax.axis_index("hour")
    low = lax.rem(s, SIDE)
    y = lax.rem(s // SIDE, YS)
    plane = lax.rem(s, PLANE)
    half = s // PLANE
    z = half * hours + h
    zs = 2 * hours
    nbins, own = coef.shape
    block = sky.shape[2]
    patches = sky_in.shape[0]
    whole = nbins // LANES * LANES

    def hour_of(d):
        return (s, lax.rem(h + d, hours))

    def low_of(d):
        return (s - low + lax.rem(low + d, SIDE), h)

    def y_of(d):
        return (half * PLANE + lax.rem(y + d, YS) * SIDE + low, h)

    def plane_of(d):
        return (half * PLANE + lax.rem(plane + d, PLANE), h)

    def z_of(d):
        there = lax.rem(z + d, zs)
        return (there // hours * PLANE + plane, lax.rem(there, hours))

    giver = ((1 - half) * PLANE + plane, (hours - 1) * (1 - h // 2))
    at_end = lax.rem(h, hours - 1) == 0
    first_taker = (hours - 1 - h) // (hours - 1) * 2

    def taker(t):
        return ((1 - half) * PLANE + plane, first_taker + t)

    barrier = pltpu.get_barrier_semaphore()
    for d in range(1, hours):
        pl.semaphore_signal(barrier, inc=1, device_id=hour_of(d), device_id_type=MESH)
    pl.semaphore_signal(barrier, inc=1, device_id=giver, device_id_type=MESH)
    for d in range(1, SIDE):
        pl.semaphore_signal(barrier, inc=1, device_id=low_of(d), device_id_type=MESH)
    for d in range(1, YS):
        pl.semaphore_signal(barrier, inc=1, device_id=y_of(d), device_id_type=MESH)

    own_columns = pl.ds(pl.multiple_of(h * own, own), own)
    small = []
    for source, held in (
        (bins_hbm, bins_ref),
        (rad_hbm, rad_ref),
        (sky_hbm, sky_in),
        (zone_hbm, zone_ref),
        (area_hbm, area_ref),
        (openness_hbm, openness_ref),
    ):
        small.append(pltpu.make_async_copy(source, held, local_sem.at[len(small)]))
    local = []
    chunk = 1024
    for at in range(0, nbins, chunk):
        rows = pl.ds(at, min(chunk, nbins - at))
        local.append((coef_hbm.at[rows], coef.at[rows]))
    local.append((open_hbm.at[:, own_columns], open_own))
    local.append((closed_hbm.at[:, own_columns], closed_own))
    local.append((target_hbm.at[:, own_columns], target.at[0]))
    local = [
        pltpu.make_async_copy(source, held, local_sem.at[len(small) + i]) for i, (source, held) in enumerate(local)
    ]
    for copy in small + local:
        copy.start()
    for copy in small:
        copy.wait()

    bins[0, 0:4, :] = bins_ref[...].astype(F32)
    bins[0, 4:8, :] = rad_ref[...].astype(F32)
    sky[0, patches // 16 * 16 :, :] = jnp.zeros_like(sky[0, patches // 16 * 16 :, :])
    sky[0, 0:patches, :] = sky_in[...]

    area = area_ref[...]
    row = lax.broadcasted_iota(jnp.int32, (SIDE, area.shape[1]), 0)
    zone_row = lax.broadcasted_iota(jnp.int32, member.shape, 0)
    member[...] = jnp.where(zone_row == zone_ref[...], 1.0, 0.0).astype(F32)
    stacked = jnp.where(
        row == 0, area * openness_ref[...], jnp.where(row == 1, area, jnp.where(row == 2, area * area, 0.0))
    )
    stat_low[0] = lax.dot_general(
        stacked, member[...], (((1,), (1,)), ((), ())), precision=HIGH, preferred_element_type=F32
    )

    lane = lax.broadcasted_iota(jnp.int32, (ROWS, LANES), 1).astype(F32)

    def build(d):
        columns[d * block : (d + 1) * block, :] = bins[d].T

        def rows_of(r, carry):
            at = pl.multiple_of(d * block + r * ROWS, ROWS)
            mine = columns[pl.ds(at, ROWS), :]
            place = [jnp.broadcast_to(mine[:, k : k + 1], (ROWS, LANES)) - lane for k in range(4)]
            value = [jnp.broadcast_to(mine[:, 4 + k : 5 + k], (ROWS, LANES)) for k in range(4)]
            for c in range(weights.shape[1] // LANES):
                first = float(c * LANES)
                w = jnp.zeros((ROWS, LANES), F32)
                for k in range(4):
                    w = jnp.where(place[k] == first, value[k], w)
                weights[pl.ds(at, ROWS), c * LANES : (c + 1) * LANES] = w.astype(BF16)
            return carry

        lax.fori_loop(0, block // ROWS, rows_of, 0)

    build(0)

    ends = 2 * (1 - lax.rem((h + 1) // 2, 2))
    pl.semaphore_wait(barrier, hours - 1 + SIDE - 1 + YS - 1 + ends)

    def remote(source, held, send, recv, device):
        return pltpu.make_async_remote_copy(
            src_ref=source, dst_ref=held, send_sem=send, recv_sem=recv, device_id=device, device_id_type=MESH
        )

    def spread(buffer, send, recv, device_of):
        copies = [
            remote(buffer.at[0], buffer.at[d], send.at[d], recv.at[d], device_of(d)) for d in range(1, buffer.shape[0])
        ]
        for copy in copies:
            copy.start()
        return copies

    def arrive(copies):
        for copy in copies:
            copy.wait_recv()

    def total_of(buffer, me):
        count = buffer.shape[0]
        total = buffer[me]
        for m in range(1, count):
            total = total + buffer[lax.rem(me + count - m, count)]
        return total

    bins_copies = spread(bins, hour_send.at[0], hour_recv.at[0], hour_of)
    stat_low_copies = spread(stat_low, low_send.at[0], low_recv.at[0], low_of)
    piece = pl.ds(pl.multiple_of(low * PIECE, PIECE), PIECE)
    sky_copies = []
    for d in range(1, hours):
        copy = remote(sky.at[0, piece], sky.at[d, piece], hour_send.at[1, d], hour_recv.at[1, d], hour_of(d))
        copy.start()
        sky_copies.append(copy)
    target_copies = []
    for d in range(1, hours):
        place = pl.ds(pl.multiple_of(lax.rem(h + d, hours) * own, own), own)
        copy = remote(target_hbm.at[:, place], target.at[d], hour_send.at[2, d], hour_recv.at[2, d], hour_of(d))
        copy.start()
        target_copies.append(copy)

    arrive(stat_low_copies)
    stat_y[0] = total_of(stat_low, low)
    stat_y_copies = spread(stat_y, y_send, y_recv, y_of)

    arrive(sky_copies)
    sky_low_copies = []
    for d in range(1, SIDE):
        held = sky.at[1:, piece]
        copy = remote(held, held, low_send.at[1, d], low_recv.at[1, d], low_of(d))
        copy.start()
        sky_low_copies.append(copy)

    arrive(bins_copies)
    for d in range(1, hours):
        build(d)
    for copy in local:
        copy.wait()
    tail_wide[...] = jnp.zeros_like(tail_wide)
    tail_wide[0 : nbins - whole, :] = coef[whole:nbins, :].astype(F32)
    tail[...] = tail_wide[...].astype(BF16)

    arrive(stat_y_copies)
    stat_half[0] = total_of(stat_y, y)
    half_copies = [
        remote(stat_half.at[0], stat_half.at[1], half_send.at[t], half_recv.at[0], taker(t)) for t in range(2)
    ]

    @pl.when(at_end)
    def _():
        for copy in half_copies:
            copy.start()

    for d in range(hours):
        here = slice(d * block, (d + 1) * block)
        cross[d] = jnp.dot(weights[here, 0:whole], coef[0:whole, :], preferred_element_type=F32) + jnp.dot(
            weights[here, whole:], tail[...], preferred_element_type=F32
        )

    arrive(sky_low_copies)
    first = (((0,), (0,)), ((), ()))
    for d in range(hours):
        op_part = lax.dot_general(sky[d, 0:patches], open_own[...], first, preferred_element_type=F32)
        cl_part = lax.dot_general(sky[d, 0:patches], closed_own[...], first, preferred_element_type=F32)
        cross[d] = op_part - cl_part + cross[d]
        lit[d] = cl_part

    half_copies[0].wait_recv()
    sums = stat_half[0] + stat_half[1]
    zone_lane = lax.broadcasted_iota(jnp.int32, (1, LANES), 1)
    den = jnp.where(zone_lane < 2 * PLANE, sums[1:2], 1.0)
    shares = sums[0:1] / den
    share = jnp.sum(jnp.where(zone_lane == s, shares, 0.0), axis=1, keepdims=True)

    lit_copies = []
    for d in (1, 2, 3, 0):
        level = lit[d] + share * cross[d]
        lit[d] = level
        lit_out[d] = level.astype(BF16)
        if d:
            held = lit_hbm.at[:, own_columns]
            copy = remote(lit_out.at[d], held, hour_send.at[3, d], hour_recv.at[3, d], hour_of(hours - d))
            copy.start()
            lit_copies.append(copy)
    own_out = pltpu.make_async_copy(lit_out.at[0], lit_hbm.at[:, own_columns], local_sem.at[0])
    own_out.start()

    terms = jnp.zeros((1, own), F32)
    for d in range(hours):
        if d:
            target_copies[d - 1].wait_recv()
        part = 2.0 * (lit[d] - target[d].astype(F32)) * cross[d]
        terms = terms + jnp.sum(part, axis=0, keepdims=True)
    local_grad = jnp.sum(terms, axis=1, keepdims=True)
    grad_z[0] = jnp.where(zone_lane == s, local_grad, 0.0)
    z_copies = spread(grad_z, z_send, z_recv, z_of)
    arrive(z_copies)
    grad_plane[0] = total_of(grad_z, z)
    plane_copies = spread(grad_plane, plane_send, plane_recv, plane_of)
    arrive(plane_copies)
    zone_grad = total_of(grad_plane, plane)
    ratio = zone_grad / den
    square = jnp.sum(ratio * ratio * sums[2:3], axis=1, keepdims=True)
    rms = jnp.sqrt(square / windows_all + 1e-06)
    spread_ratio = jnp.dot(
        jnp.broadcast_to(ratio, (SIDE, LANES)), member[...], precision=HIGH, preferred_element_type=F32
    )
    grad = area_ref[...] * spread_ratio[0:1]
    new_ref[...] = jnp.clip(openness_ref[...] - 0.25 * grad / rms, 0.0, 1.0)

    for copy in bins_copies + stat_low_copies + sky_copies + target_copies + stat_y_copies + sky_low_copies:
        copy.wait_send()
    for copy in z_copies + plane_copies:
        copy.wait_send()

    @pl.when(at_end)
    def _():
        for copy in half_copies:
            copy.wait_send()

    own_out.wait()
    for copy in lit_copies:
        copy.wait()


def solution(mesh):
    hours = mesh.shape["hour"]
    sens = mesh.shape["sens"]

    def step(sky, sky_open, sky_closed, sun_coef, sun_bins, sun_rad, target, zone_of, area, openness):
        block, patches = sky.shape
        nbins, own = sun_coef.shape
        windows = area.shape[0]
        padded = pl.cdiv(nbins, LANES) * LANES
        any_space = pl.BlockSpec(memory_space=pl.ANY)
        hbm = pl.BlockSpec(memory_space=pltpu.HBM)
        vmem = pl.BlockSpec(memory_space=pltpu.VMEM)
        tile = (SIDE, LANES)
        lit, new = pl.pallas_call(
            functools.partial(kernel, hours, windows * sens),
            out_shape=(
                jax.ShapeDtypeStruct((block, own * hours), BF16),
                jax.ShapeDtypeStruct((1, windows), F32),
            ),
            in_specs=[hbm] * 10,
            out_specs=(any_space, vmem),
            scratch_shapes=[
                pltpu.VMEM(sun_bins.T.shape, jnp.int32),
                pltpu.VMEM(sun_rad.T.shape, BF16),
                pltpu.VMEM((1, windows), jnp.int32),
                pltpu.VMEM((1, windows), F32),
                pltpu.VMEM((1, windows), F32),
                pltpu.VMEM((nbins, own), BF16),
                pltpu.VMEM((LANES, own), F32),
                pltpu.VMEM((LANES, own), BF16),
                pltpu.VMEM((hours * block, padded), BF16),
                pltpu.VMEM((hours * block, SIDE), F32),
                pltpu.VMEM((hours,) + tile, F32),
                pltpu.VMEM((patches, block), BF16),
                pltpu.VMEM((hours, SIDE * PIECE, block), BF16),
                pltpu.VMEM((hours, block, own), BF16),
                pltpu.VMEM((patches, own), BF16),
                pltpu.VMEM((patches, own), BF16),
                pltpu.VMEM((hours, block, own), F32),
                pltpu.VMEM((hours, block, own), F32),
                pltpu.VMEM((hours, block, own), BF16),
                pltpu.VMEM((LANES, windows), F32),
                pltpu.VMEM((SIDE,) + tile, F32),
                pltpu.VMEM((YS,) + tile, F32),
                pltpu.VMEM((2,) + tile, F32),
                pltpu.VMEM((2 * hours, 1, LANES), F32),
                pltpu.VMEM((PLANE, 1, LANES), F32),
                pltpu.SemaphoreType.DMA((16,)),
                pltpu.SemaphoreType.DMA((4, hours)),
                pltpu.SemaphoreType.DMA((4, hours)),
                pltpu.SemaphoreType.DMA((2, SIDE)),
                pltpu.SemaphoreType.DMA((2, SIDE)),
                pltpu.SemaphoreType.DMA((YS,)),
                pltpu.SemaphoreType.DMA((YS,)),
                pltpu.SemaphoreType.DMA((2,)),
                pltpu.SemaphoreType.DMA((1,)),
                pltpu.SemaphoreType.DMA((2 * hours,)),
                pltpu.SemaphoreType.DMA((2 * hours,)),
                pltpu.SemaphoreType.DMA((PLANE,)),
                pltpu.SemaphoreType.DMA((PLANE,)),
            ],
            compiler_params=pltpu.CompilerParams(
                collective_id=0, has_side_effects=True, vmem_limit_bytes=48 << 20
            ),
        )(
            *(
                pltpu.with_memory_space_constraint(x, pltpu.HBM)
                for x in (
                    sky.T,
                    sky_open,
                    sky_closed,
                    sun_coef,
                    sun_bins.T,
                    sun_rad.T,
                    target,
                    zone_of.T,
                    area[None, :],
                    openness[None, :],
                )
            )
        )
        return lit, new[0]

    in_specs = (
        P("hour", None),
        P(None, "sens"),
        P(None, "sens"),
        P(None, ("sens", "hour")),
        P("hour", None),
        P("hour", None),
        P("hour", "sens"),
        P("sens", None),
        P("sens"),
        P("sens"),
    )
    out_specs = (P("hour", "sens"), P("sens"))
    return jax.shard_map(step, mesh=mesh, in_specs=in_specs, out_specs=out_specs, check_vma=False)
```

time: 60.7 us -> 47.3 us (0.78)
  local copies, waits for them, and re-layouts: 8.77 us -> 1.39 us
  Pallas kernels: 50.9 us -> 45.1 us
    unnamed x20 -> x2, local copies, waits for them, and re-layouts: 8.77 us -> 1.39 us
    pallas_call x1, Pallas kernels: 50.9 us -> 45.1 us  [step(): pl.pallas_call(functools.partial(kernel, hours, windows * sens), out_shap...]
where the time goes in v2:
time: 47.3 us; the launch traced here: 47.2 us
  Pallas kernels  45.1 us (95%)
  local copies, waits for them, and re-layouts  1.39 us (3%)
  between operations  0.64 us (1%)
    pallas_call x1, Pallas kernels, step(): pl.pallas_call(functools.partial(kernel, hours, windows * sens), out_shap...  45.1 us
    unnamed x2, local copies, waits for them, and re-layouts  1.39 us

profile of v2, /device:TPU:1, one launch (start us, length us, event | category | flops | bytes accessed | tf_op | source)
XLA Modules:
  0.0 47.2 jit_solution(2622295034097356103)
XLA Ops:
  0.6 45.1 %shard_map.113 = (bf16[128,2048]{1,0:T(8,128)(2,1)S(1)}, f32[1,1024]{1,0:T(1,128)S(1)}) custom-call(bf16[146,128]{1,0:T(8,128)(2,1)} %bitcast.8, bf16[146,2048]{1,0:T(8,128)(2,1)} %open_hbm.1, bf16[146,2048]{1,0:T(8,128)(2,1)} %closed_hbm.1, bf16[5165,512]{1,0:T(8,128)(2,1)} %coef_hbm.1, s32[4,128]{1,0:T(4,128)} %bitcast.12, bf16[4,128]{1,0:T(4,128)(2,1)} %bitcast.13, ...), custom_call_target="tpu_custom_call" | custom-call | tf_op jit(solution)/shard_map/pallas_call | solution.py:345
  45.8 0.8 %copy.14 = bf16[128,2048]{1,0:T(8,128)(2,1)} copy(bf16[128,2048]{1,0:T(8,128)(2,1)S(1)} %get-tuple-element.8) | data formatting | bytes 1048576
  46.6 0.6 %copy.15 = f32[1024]{0:T(1024)} copy(f32[1024]{0:T(1024)S(1)} %bitcast.7) | data formatting | bytes 8192

commit v3 on v2

--- a/solution.py
+++ b/solution.py
@@ -13,6 +13,7 @@
 HIGH = lax.Precision.HIGHEST
 SIDE = 8
 YS = 4
+CORES = 2
 PLANE = SIDE * YS
 PIECE = 24
 LANES = 128
@@ -54,11 +55,11 @@
     lit,
     lit_out,
     member,
+    member_half,
     stat_low,
-    stat_y,
-    stat_half,
-    grad_z,
-    grad_plane,
+    stat_all,
+    grad_column,
+    grad_all,
     local_sem,
     hour_send,
     hour_recv,
@@ -68,10 +69,11 @@
     y_recv,
     half_send,
     half_recv,
-    z_send,
-    z_recv,
-    plane_send,
-    plane_recv,
+    column_send,
+    column_recv,
+    across_send,
+    across_recv,
+    y_ready,
 ):
     s = lax.axis_index("sens")
     h = lax.axis_index("hour")
@@ -95,19 +97,24 @@
     def y_of(d):
         return (half * PLANE + lax.rem(y + d, YS) * SIDE + low, h)
 
-    def plane_of(d):
-        return (half * PLANE + lax.rem(plane + d, PLANE), h)
-
-    def z_of(d):
-        there = lax.rem(z + d, zs)
-        return (there // hours * PLANE + plane, lax.rem(there, hours))
+    core = lax.rem(s, CORES)
+    in_column = z * CORES + core
+    chip = plane // CORES
+
+    def column_of(d):
+        there = lax.rem(in_column + d, zs * CORES)
+        there_z = there // CORES
+        return (there_z // hours * PLANE + chip * CORES + lax.rem(there, CORES), lax.rem(there_z, hours))
+
+    def across_of(d):
+        return (half * PLANE + lax.rem(chip + d, PLANE // CORES) * CORES + core, h)
 
     giver = ((1 - half) * PLANE + plane, (hours - 1) * (1 - h // 2))
     at_end = lax.rem(h, hours - 1) == 0
     first_taker = (hours - 1 - h) // (hours - 1) * 2
 
-    def taker(t):
-        return ((1 - half) * PLANE + plane, first_taker + t)
+    def taker(t, there_y):
+        return ((1 - half) * PLANE + there_y * SIDE + low, first_taker + t)
 
     barrier = pltpu.get_barrier_semaphore()
     for d in range(1, hours):
@@ -154,10 +161,11 @@
     row = lax.broadcasted_iota(jnp.int32, (SIDE, area.shape[1]), 0)
     zone_row = lax.broadcasted_iota(jnp.int32, member.shape, 0)
     member[...] = jnp.where(zone_row == zone_ref[...], 1.0, 0.0).astype(F32)
+    member_half[...] = member[...].astype(BF16)
     stacked = jnp.where(
         row == 0, area * openness_ref[...], jnp.where(row == 1, area, jnp.where(row == 2, area * area, 0.0))
     )
-    stat_low[0] = lax.dot_general(
+    stat_low[low] = lax.dot_general(
         stacked, member[...], (((1,), (1,)), ((), ())), precision=HIGH, preferred_element_type=F32
     )
 
@@ -191,10 +199,9 @@
             src_ref=source, dst_ref=held, send_sem=send, recv_sem=recv, device_id=device, device_id_type=MESH
         )
 
-    def spread(buffer, send, recv, device_of):
-        copies = [
-            remote(buffer.at[0], buffer.at[d], send.at[d], recv.at[d], device_of(d)) for d in range(1, buffer.shape[0])
-        ]
+    def spread(buffer, me, send, recv, device_of):
+        mine = buffer.at[me]
+        copies = [remote(mine, mine, send.at[d], recv.at[d], device_of(d)) for d in range(1, buffer.shape[0])]
         for copy in copies:
             copy.start()
         return copies
@@ -203,15 +210,20 @@
         for copy in copies:
             copy.wait_recv()
 
-    def total_of(buffer, me):
-        count = buffer.shape[0]
-        total = buffer[me]
-        for m in range(1, count):
-            total = total + buffer[lax.rem(me + count - m, count)]
+    def total_of(buffer):
+        total = buffer[0]
+        for m in range(1, buffer.shape[0]):
+            total = total + buffer[m]
         return total
 
-    bins_copies = spread(bins, hour_send.at[0], hour_recv.at[0], hour_of)
-    stat_low_copies = spread(stat_low, low_send.at[0], low_recv.at[0], low_of)
+    stat_low_copies = spread(stat_low, low, low_send.at[0], low_recv.at[0], low_of)
+    for d in range(1, YS):
+        pl.semaphore_signal(y_ready, inc=1, device_id=y_of(d), device_id_type=MESH)
+    bins_copies = []
+    for d in range(1, hours):
+        copy = remote(bins.at[0], bins.at[d], hour_send.at[0, d], hour_recv.at[0, d], hour_of(d))
+        copy.start()
+        bins_copies.append(copy)
     piece = pl.ds(pl.multiple_of(low * PIECE, PIECE), PIECE)
     sky_copies = []
     for d in range(1, hours):
@@ -226,8 +238,25 @@
         target_copies.append(copy)
 
     arrive(stat_low_copies)
-    stat_y[0] = total_of(stat_low, low)
-    stat_y_copies = spread(stat_y, y_send, y_recv, y_of)
+    group = half * YS + y
+    stat_all[group] = total_of(stat_low)
+    mine = stat_all.at[group]
+    stat_y_copies = []
+    for d in range(1, YS):
+        copy = remote(mine, mine, y_send.at[d], y_recv.at[d], y_of(d))
+        copy.start()
+        stat_y_copies.append(copy)
+    pl.semaphore_wait(y_ready, YS - 1)
+    half_copies = [
+        remote(mine, mine, half_send.at[t, there_y], half_recv.at[y], taker(t, there_y))
+        for there_y in range(YS)
+        for t in range(2)
+    ]
+
+    @pl.when(at_end)
+    def _():
+        for copy in half_copies:
+            copy.start()
 
     arrive(sky_copies)
     sky_low_copies = []
@@ -245,17 +274,6 @@
     tail_wide[...] = jnp.zeros_like(tail_wide)
     tail_wide[0 : nbins - whole, :] = coef[whole:nbins, :].astype(F32)
     tail[...] = tail_wide[...].astype(BF16)
-
-    arrive(stat_y_copies)
-    stat_half[0] = total_of(stat_y, y)
-    half_copies = [
-        remote(stat_half.at[0], stat_half.at[1], half_send.at[t], half_recv.at[0], taker(t)) for t in range(2)
-    ]
-
-    @pl.when(at_end)
-    def _():
-        for copy in half_copies:
-            copy.start()
 
     for d in range(hours):
         here = slice(d * block, (d + 1) * block)
@@ -271,23 +289,19 @@
         cross[d] = op_part - cl_part + cross[d]
         lit[d] = cl_part
 
-    half_copies[0].wait_recv()
-    sums = stat_half[0] + stat_half[1]
+    arrive(stat_y_copies)
+    for there_y in range(YS):
+        remote(mine, mine, half_send.at[0, 0], half_recv.at[there_y], taker(0, 0)).wait_recv()
+    sums = total_of(stat_all)
     zone_lane = lax.broadcasted_iota(jnp.int32, (1, LANES), 1)
     den = jnp.where(zone_lane < 2 * PLANE, sums[1:2], 1.0)
     shares = sums[0:1] / den
     share = jnp.sum(jnp.where(zone_lane == s, shares, 0.0), axis=1, keepdims=True)
 
-    lit_copies = []
-    for d in (1, 2, 3, 0):
+    for d in range(hours):
         level = lit[d] + share * cross[d]
         lit[d] = level
         lit_out[d] = level.astype(BF16)
-        if d:
-            held = lit_hbm.at[:, own_columns]
-            copy = remote(lit_out.at[d], held, hour_send.at[3, d], hour_recv.at[3, d], hour_of(hours - d))
-            copy.start()
-            lit_copies.append(copy)
     own_out = pltpu.make_async_copy(lit_out.at[0], lit_hbm.at[:, own_columns], local_sem.at[0])
     own_out.start()
 
@@ -298,25 +312,36 @@
         part = 2.0 * (lit[d] - target[d].astype(F32)) * cross[d]
         terms = terms + jnp.sum(part, axis=0, keepdims=True)
     local_grad = jnp.sum(terms, axis=1, keepdims=True)
-    grad_z[0] = jnp.where(zone_lane == s, local_grad, 0.0)
-    z_copies = spread(grad_z, z_send, z_recv, z_of)
-    arrive(z_copies)
-    grad_plane[0] = total_of(grad_z, z)
-    plane_copies = spread(grad_plane, plane_send, plane_recv, plane_of)
-    arrive(plane_copies)
-    zone_grad = total_of(grad_plane, plane)
+    grad_column[in_column] = jnp.where(zone_lane == s, local_grad, 0.0)
+    column_copies = spread(grad_column, in_column, column_send, column_recv, column_of)
+    lit_copies = []
+    for d in range(1, hours):
+        held = lit_hbm.at[:, own_columns]
+        copy = remote(lit_out.at[d], held, hour_send.at[3, d], hour_recv.at[3, d], hour_of(hours - d))
+        copy.start()
+        lit_copies.append(copy)
+    arrive(column_copies)
+    grad_all[chip] = total_of(grad_column)
+    across_copies = spread(grad_all, chip, across_send, across_recv, across_of)
+    arrive(across_copies)
+    zone_grad = total_of(grad_all)
     ratio = zone_grad / den
     square = jnp.sum(ratio * ratio * sums[2:3], axis=1, keepdims=True)
     rms = jnp.sqrt(square / windows_all + 1e-06)
-    spread_ratio = jnp.dot(
-        jnp.broadcast_to(ratio, (SIDE, LANES)), member[...], precision=HIGH, preferred_element_type=F32
-    )
-    grad = area_ref[...] * spread_ratio[0:1]
+    first_part = ratio.astype(BF16).astype(F32)
+    second_part = (ratio - first_part).astype(BF16).astype(F32)
+    third_part = ratio - first_part - second_part
+    part_row = lax.broadcasted_iota(jnp.int32, (16, LANES), 0)
+    parts = jnp.where(part_row == 0, first_part, jnp.where(part_row == 1, second_part, third_part))
+    parts = jnp.where(part_row < 3, parts, 0.0).astype(BF16)
+    chosen = jnp.dot(parts, member_half[...], preferred_element_type=F32)
+    chosen = chosen[0:1] + chosen[1:2] + chosen[2:3]
+    grad = area_ref[...] * chosen
     new_ref[...] = jnp.clip(openness_ref[...] - 0.25 * grad / rms, 0.0, 1.0)
 
     for copy in bins_copies + stat_low_copies + sky_copies + target_copies + stat_y_copies + sky_low_copies:
         copy.wait_send()
-    for copy in z_copies + plane_copies:
+    for copy in column_copies + across_copies:
         copy.wait_send()
 
     @pl.when(at_end)
@@ -371,11 +396,11 @@
                 pltpu.VMEM((hours, block, own), F32),
                 pltpu.VMEM((hours, block, own), BF16),
                 pltpu.VMEM((LANES, windows), F32),
+                pltpu.VMEM((LANES, windows), BF16),
                 pltpu.VMEM((SIDE,) + tile, F32),
-                pltpu.VMEM((YS,) + tile, F32),
-                pltpu.VMEM((2,) + tile, F32),
-                pltpu.VMEM((2 * hours, 1, LANES), F32),
-                pltpu.VMEM((PLANE, 1, LANES), F32),
+                pltpu.VMEM((2 * YS,) + tile, F32),
+                pltpu.VMEM((2 * hours * CORES, 1, LANES), F32),
+                pltpu.VMEM((PLANE // CORES, 1, LANES), F32),
                 pltpu.SemaphoreType.DMA((16,)),
                 pltpu.SemaphoreType.DMA((4, hours)),
                 pltpu.SemaphoreType.DMA((4, hours)),
@@ -383,12 +408,13 @@
                 pltpu.SemaphoreType.DMA((2, SIDE)),
                 pltpu.SemaphoreType.DMA((YS,)),
                 pltpu.SemaphoreType.DMA((YS,)),
-                pltpu.SemaphoreType.DMA((2,)),
-                pltpu.SemaphoreType.DMA((1,)),
-                pltpu.SemaphoreType.DMA((2 * hours,)),
-                pltpu.SemaphoreType.DMA((2 * hours,)),
-                pltpu.SemaphoreType.DMA((PLANE,)),
-                pltpu.SemaphoreType.DMA((PLANE,)),
+                pltpu.SemaphoreType.DMA((2, YS)),
+                pltpu.SemaphoreType.DMA((YS,)),
+                pltpu.SemaphoreType.DMA((2 * hours * CORES,)),
+                pltpu.SemaphoreType.DMA((2 * hours * CORES,)),
+                pltpu.SemaphoreType.DMA((PLANE // CORES,)),
+                pltpu.SemaphoreType.DMA((PLANE // CORES,)),
+                pltpu.SemaphoreType.REGULAR,
             ],
             compiler_params=pltpu.CompilerParams(
                 collective_id=0, has_side_effects=True, vmem_limit_bytes=48 << 20

time: 47.3 us -> 37.8 us (0.80)
  Pallas kernels: 45.1 us -> 35.7 us
    pallas_call x1, Pallas kernels: 45.1 us -> 35.7 us  [step(): pl.pallas_call(functools.partial(kernel, hours, windows * sens), out_shap...]
where the time goes in v3:
time: 37.8 us; the launch traced here: 37.7 us
  Pallas kernels  35.7 us (94%)
  local copies, waits for them, and re-layouts  1.39 us (4%)
  between operations  0.64 us (2%)
    pallas_call x1, Pallas kernels, step(): pl.pallas_call(functools.partial(kernel, hours, windows * sens), out_shap...  35.7 us
    unnamed x2, local copies, waits for them, and re-layouts  1.39 us

profile of v3, /device:TPU:1, one launch (start us, length us, event | category | flops | bytes accessed | tf_op | source)
XLA Modules:
  0.0 37.7 jit_solution(12882061178771647236)
XLA Ops:
  0.6 35.7 %shard_map.113 = (bf16[128,2048]{1,0:T(8,128)(2,1)S(1)}, f32[1,1024]{1,0:T(1,128)S(1)}) custom-call(bf16[146,128]{1,0:T(8,128)(2,1)} %bitcast.8, bf16[146,2048]{1,0:T(8,128)(2,1)} %open_hbm.1, bf16[146,2048]{1,0:T(8,128)(2,1)} %closed_hbm.1, bf16[5165,512]{1,0:T(8,128)(2,1)} %coef_hbm.1, s32[4,128]{1,0:T(4,128)} %bitcast.12, bf16[4,128]{1,0:T(4,128)(2,1)} %bitcast.13, ...), custom_call_target="tpu_custom_call" | custom-call | tf_op jit(solution)/shard_map/pallas_call | solution.py:370
  36.3 0.8 %copy.14 = bf16[128,2048]{1,0:T(8,128)(2,1)} copy(bf16[128,2048]{1,0:T(8,128)(2,1)S(1)} %get-tuple-element.8) | data formatting | bytes 1048576
  37.1 0.6 %copy.15 = f32[1024]{0:T(1024)} copy(f32[1024]{0:T(1024)S(1)} %bitcast.7) | data formatting | bytes 8192

commit v4 on v3

--- a/solution.py
+++ b/solution.py
@@ -14,6 +14,7 @@
 SIDE = 8
 YS = 4
 CORES = 2
+XS = 4
 PLANE = SIDE * YS
 PIECE = 24
 LANES = 128
@@ -55,7 +56,6 @@
     lit,
     lit_out,
     member,
-    member_half,
     stat_low,
     stat_all,
     grad_column,
@@ -78,9 +78,9 @@
     s = lax.axis_index("sens")
     h = lax.axis_index("hour")
     low = lax.rem(s, SIDE)
-    y = lax.rem(s // SIDE, YS)
+    y = lax.rem(lax.div(s, SIDE), YS)
     plane = lax.rem(s, PLANE)
-    half = s // PLANE
+    half = lax.div(s, PLANE)
     z = half * hours + h
     zs = 2 * hours
     nbins, own = coef.shape
@@ -99,19 +99,24 @@
 
     core = lax.rem(s, CORES)
     in_column = z * CORES + core
-    chip = plane // CORES
+    chip = lax.div(plane, CORES)
+    chip_x = lax.rem(chip, XS)
+    columns_z = [lax.rem(z + d, zs) for d in range(zs)]
+    columns_z = [(lax.div(there, hours) * PLANE + chip * CORES, lax.rem(there, hours)) for there in columns_z]
+    columns_core = [core, 1 - core]
+    across_y = [half * PLANE + lax.rem(y + d, YS) * SIDE + core for d in range(YS)]
+    across_x = [lax.rem(chip_x + d, XS) * CORES for d in range(XS)]
 
     def column_of(d):
-        there = lax.rem(in_column + d, zs * CORES)
-        there_z = there // CORES
-        return (there_z // hours * PLANE + chip * CORES + lax.rem(there, CORES), lax.rem(there_z, hours))
+        first, there = columns_z[d // CORES]
+        return (first + columns_core[d % CORES], there)
 
     def across_of(d):
-        return (half * PLANE + lax.rem(chip + d, PLANE // CORES) * CORES + core, h)
-
-    giver = ((1 - half) * PLANE + plane, (hours - 1) * (1 - h // 2))
+        return (across_y[d // XS] + across_x[d % XS], h)
+
+    giver = ((1 - half) * PLANE + plane, (hours - 1) * (1 - lax.div(h, 2)))
     at_end = lax.rem(h, hours - 1) == 0
-    first_taker = (hours - 1 - h) // (hours - 1) * 2
+    first_taker = lax.div(hours - 1 - h, hours - 1) * 2
 
     def taker(t, there_y):
         return ((1 - half) * PLANE + there_y * SIDE + low, first_taker + t)
@@ -149,25 +154,13 @@
     ]
     for copy in small + local:
         copy.start()
-    for copy in small:
+    for copy in small[:3]:
         copy.wait()
 
     bins[0, 0:4, :] = bins_ref[...].astype(F32)
     bins[0, 4:8, :] = rad_ref[...].astype(F32)
     sky[0, patches // 16 * 16 :, :] = jnp.zeros_like(sky[0, patches // 16 * 16 :, :])
     sky[0, 0:patches, :] = sky_in[...]
-
-    area = area_ref[...]
-    row = lax.broadcasted_iota(jnp.int32, (SIDE, area.shape[1]), 0)
-    zone_row = lax.broadcasted_iota(jnp.int32, member.shape, 0)
-    member[...] = jnp.where(zone_row == zone_ref[...], 1.0, 0.0).astype(F32)
-    member_half[...] = member[...].astype(BF16)
-    stacked = jnp.where(
-        row == 0, area * openness_ref[...], jnp.where(row == 1, area, jnp.where(row == 2, area * area, 0.0))
-    )
-    stat_low[low] = lax.dot_general(
-        stacked, member[...], (((1,), (1,)), ((), ())), precision=HIGH, preferred_element_type=F32
-    )
 
     lane = lax.broadcasted_iota(jnp.int32, (ROWS, LANES), 1).astype(F32)
 
@@ -189,9 +182,7 @@
 
         lax.fori_loop(0, block // ROWS, rows_of, 0)
 
-    build(0)
-
-    ends = 2 * (1 - lax.rem((h + 1) // 2, 2))
+    ends = 2 * (1 - lax.rem(lax.div(h + 1, 2), 2))
     pl.semaphore_wait(barrier, hours - 1 + SIDE - 1 + YS - 1 + ends)
 
     def remote(source, held, send, recv, device):
@@ -216,26 +207,70 @@
             total = total + buffer[m]
         return total
 
+    bins_copies = []
+    for d in range(1, hours):
+        copy = remote(bins.at[0], bins.at[d], hour_send.at[0, d], hour_recv.at[0, d], hour_of(d))
+        copy.start()
+        bins_copies.append(copy)
+    piece = pl.ds(pl.multiple_of(low * PIECE, PIECE), PIECE)
+    sky_copies = []
+    for d in range(1, hours):
+        copy = remote(sky.at[0, piece], sky.at[d, piece], hour_send.at[1, d], hour_recv.at[1, d], hour_of(d))
+        copy.start()
+        sky_copies.append(copy)
+    target_copies = []
+    for d in range(1, hours):
+        place = pl.ds(pl.multiple_of(lax.rem(h + d, hours) * own, own), own)
+        copy = remote(target_hbm.at[:, place], target.at[d], hour_send.at[2, d], hour_recv.at[2, d], hour_of(d))
+        copy.start()
+        target_copies.append(copy)
+
+    for copy in small[3:]:
+        copy.wait()
+    area = area_ref[...]
+    zone_row = lax.broadcasted_iota(jnp.int32, member.shape, 0)
+    member[...] = jnp.where(zone_row == zone_ref[...], 1.0, 0.0).astype(BF16)
+
+    def parts_of(value):
+        first = value.astype(BF16).astype(F32)
+        second = (value - first).astype(BF16).astype(F32)
+        return first, second, value - first - second
+
+    row = lax.broadcasted_iota(jnp.int32, (16, area.shape[1]), 0)
+    stacked = jnp.zeros(row.shape, F32)
+    for i, value in enumerate((area * openness_ref[...], area, area * area)):
+        for part, rest in enumerate(parts_of(value)):
+            stacked = jnp.where(row == 4 * part + i, rest, stacked)
+    partial = lax.dot_general(
+        stacked.astype(BF16), member[...], (((1,), (1,)), ((), ())), preferred_element_type=F32
+    )
+    stat_low[low, 0:4] = partial[0:4] + partial[4:8] + partial[8:12]
+    stat_low[low, 4:8] = jnp.zeros((4, LANES), F32)
+
     stat_low_copies = spread(stat_low, low, low_send.at[0], low_recv.at[0], low_of)
     for d in range(1, YS):
         pl.semaphore_signal(y_ready, inc=1, device_id=y_of(d), device_id_type=MESH)
-    bins_copies = []
-    for d in range(1, hours):
-        copy = remote(bins.at[0], bins.at[d], hour_send.at[0, d], hour_recv.at[0, d], hour_of(d))
-        copy.start()
-        bins_copies.append(copy)
-    piece = pl.ds(pl.multiple_of(low * PIECE, PIECE), PIECE)
-    sky_copies = []
-    for d in range(1, hours):
-        copy = remote(sky.at[0, piece], sky.at[d, piece], hour_send.at[1, d], hour_recv.at[1, d], hour_of(d))
-        copy.start()
-        sky_copies.append(copy)
-    target_copies = []
-    for d in range(1, hours):
-        place = pl.ds(pl.multiple_of(lax.rem(h + d, hours) * own, own), own)
-        copy = remote(target_hbm.at[:, place], target.at[d], hour_send.at[2, d], hour_recv.at[2, d], hour_of(d))
-        copy.start()
-        target_copies.append(copy)
+    def sun_of(d):
+        here = slice(d * block, (d + 1) * block)
+        cross[d] = jnp.dot(weights[here, 0:whole], coef[0:whole, :], preferred_element_type=F32) + jnp.dot(
+            weights[here, whole:], tail[...], preferred_element_type=F32
+        )
+
+    def levels_of(d):
+        first = (((0,), (0,)), ((), ()))
+        op_part = lax.dot_general(sky[d, 0:patches], open_own[...], first, preferred_element_type=F32)
+        cl_part = lax.dot_general(sky[d, 0:patches], closed_own[...], first, preferred_element_type=F32)
+        cross[d] = op_part - cl_part + cross[d]
+        lit[d] = cl_part
+
+    build(0)
+    for copy in local:
+        copy.wait()
+    tail_wide[...] = jnp.zeros_like(tail_wide)
+    tail_wide[0 : nbins - whole, :] = coef[whole:nbins, :].astype(F32)
+    tail[...] = tail_wide[...].astype(BF16)
+    sun_of(0)
+    levels_of(0)
 
     arrive(stat_low_copies)
     group = half * YS + y
@@ -269,25 +304,11 @@
     arrive(bins_copies)
     for d in range(1, hours):
         build(d)
-    for copy in local:
-        copy.wait()
-    tail_wide[...] = jnp.zeros_like(tail_wide)
-    tail_wide[0 : nbins - whole, :] = coef[whole:nbins, :].astype(F32)
-    tail[...] = tail_wide[...].astype(BF16)
-
-    for d in range(hours):
-        here = slice(d * block, (d + 1) * block)
-        cross[d] = jnp.dot(weights[here, 0:whole], coef[0:whole, :], preferred_element_type=F32) + jnp.dot(
-            weights[here, whole:], tail[...], preferred_element_type=F32
-        )
-
+    for d in range(1, hours):
+        sun_of(d)
     arrive(sky_low_copies)
-    first = (((0,), (0,)), ((), ()))
-    for d in range(hours):
-        op_part = lax.dot_general(sky[d, 0:patches], open_own[...], first, preferred_element_type=F32)
-        cl_part = lax.dot_general(sky[d, 0:patches], closed_own[...], first, preferred_element_type=F32)
-        cross[d] = op_part - cl_part + cross[d]
-        lit[d] = cl_part
+    for d in range(1, hours):
+        levels_of(d)
 
     arrive(stat_y_copies)
     for there_y in range(YS):
@@ -328,13 +349,11 @@
     ratio = zone_grad / den
     square = jnp.sum(ratio * ratio * sums[2:3], axis=1, keepdims=True)
     rms = jnp.sqrt(square / windows_all + 1e-06)
-    first_part = ratio.astype(BF16).astype(F32)
-    second_part = (ratio - first_part).astype(BF16).astype(F32)
-    third_part = ratio - first_part - second_part
+    first_part, second_part, third_part = parts_of(ratio)
     part_row = lax.broadcasted_iota(jnp.int32, (16, LANES), 0)
     parts = jnp.where(part_row == 0, first_part, jnp.where(part_row == 1, second_part, third_part))
     parts = jnp.where(part_row < 3, parts, 0.0).astype(BF16)
-    chosen = jnp.dot(parts, member_half[...], preferred_element_type=F32)
+    chosen = jnp.dot(parts, member[...], preferred_element_type=F32)
     chosen = chosen[0:1] + chosen[1:2] + chosen[2:3]
     grad = area_ref[...] * chosen
     new_ref[...] = jnp.clip(openness_ref[...] - 0.25 * grad / rms, 0.0, 1.0)
@@ -351,6 +370,14 @@
 
     own_out.wait()
     for copy in lit_copies:
+        copy.wait()
+
+
+def hand_over(lit_in, new_in, lit_hbm, new_hbm, sem):
+    copies = [pltpu.make_async_copy(lit_in, lit_hbm, sem.at[0]), pltpu.make_async_copy(new_in, new_hbm, sem.at[1])]
+    for copy in copies:
+        copy.start()
+    for copy in copies:
         copy.wait()
 
 
@@ -395,7 +422,6 @@
                 pltpu.VMEM((hours, block, own), F32),
                 pltpu.VMEM((hours, block, own), F32),
                 pltpu.VMEM((hours, block, own), BF16),
-                pltpu.VMEM((LANES, windows), F32),
                 pltpu.VMEM((LANES, windows), BF16),
                 pltpu.VMEM((SIDE,) + tile, F32),
                 pltpu.VMEM((2 * YS,) + tile, F32),
@@ -436,6 +462,14 @@
                 )
             )
         )
+        lit, new = pl.pallas_call(
+            hand_over,
+            out_shape=(jax.ShapeDtypeStruct(lit.shape, BF16), jax.ShapeDtypeStruct(new.shape, F32)),
+            in_specs=[vmem, vmem],
+            out_specs=(any_space, any_space),
+            scratch_shapes=[pltpu.SemaphoreType.DMA((2,))],
+            compiler_params=pltpu.CompilerParams(vmem_limit_bytes=1 << 20),
+        )(lit, new)
         return lit, new[0]
 
     in_specs = (

time: 37.8 us -> 37.7 us (level)
  local copies, waits for them, and re-layouts: 1.39 us -> 0 us
  Pallas kernels: 35.7 us -> 37 us
    unnamed x2 -> x0, local copies, waits for them, and re-layouts: 1.39 us -> none
    pallas_call x0 -> x1, Pallas kernels: none -> 0.81 us  [step(): pl.pallas_call(hand_over, out_shape=(jax.ShapeDtypeStruct(lit.shape, BF16...]
    pallas_call x1, Pallas kernels: 35.7 us -> 36.1 us  [step(): pl.pallas_call(functools.partial(kernel, hours, windows * sens), out_shap...]
where the time goes in v4:
time: 37.7 us; the launch traced here: 37.6 us
  Pallas kernels  37 us (98%)
  between operations  0.64 us (2%)
    pallas_call x1, Pallas kernels, step(): pl.pallas_call(functools.partial(kernel, hours, windows * sens), out_shap...  36.1 us
    pallas_call x1, Pallas kernels, step(): pl.pallas_call(hand_over, out_shape=(jax.ShapeDtypeStruct(lit.shape, BF16...  0.81 us

profile of v4, /device:TPU:1, one launch (start us, length us, event | category | flops | bytes accessed | tf_op | source)
XLA Modules:
  0.0 37.6 jit_solution(4973034037628856910)
XLA Ops:
  0.6 36.1 %shard_map.113 = (bf16[128,2048]{1,0:T(8,128)(2,1)S(1)}, f32[1,1024]{1,0:T(1,128)S(1)}) custom-call(bf16[146,128]{1,0:T(8,128)(2,1)} %bitcast.7, bf16[146,2048]{1,0:T(8,128)(2,1)} %open_hbm.1, bf16[146,2048]{1,0:T(8,128)(2,1)} %closed_hbm.1, bf16[5165,512]{1,0:T(8,128)(2,1)} %coef_hbm.1, s32[4,128]{1,0:T(4,128)} %bitcast.11, bf16[4,128]{1,0:T(4,128)(2,1)} %bitcast.12, ...), custom_call_target="tpu_custom_call" | custom-call | tf_op jit(solution)/shard_map/pallas_call | solution.py:397
  36.8 0.8 %shard_map.114 = (bf16[128,2048]{1,0:T(8,128)(2,1)}, f32[1,1024]{1,0:T(1,128)}) custom-call(bf16[128,2048]{1,0:T(8,128)(2,1)S(1)} %get-tuple-element.6.lit_in, f32[1,1024]{1,0:T(1,128)S(1)} %get-tuple-element.7.new_in), custom_call_target="tpu_custom_call" | custom-call | tf_op jit(solution)/shard_map/pallas_call | solution.py:465

commit v5 on v4

--- a/solution.py
+++ b/solution.py
@@ -162,6 +162,28 @@
     sky[0, patches // 16 * 16 :, :] = jnp.zeros_like(sky[0, patches // 16 * 16 :, :])
     sky[0, 0:patches, :] = sky_in[...]
 
+    for copy in small[3:]:
+        copy.wait()
+    area = area_ref[...]
+    zone_row = lax.broadcasted_iota(jnp.int32, member.shape, 0)
+    member[...] = jnp.where(zone_row == zone_ref[...], 1.0, 0.0).astype(BF16)
+
+    def parts_of(value):
+        first = value.astype(BF16).astype(F32)
+        second = (value - first).astype(BF16).astype(F32)
+        return first, second, value - first - second
+
+    row = lax.broadcasted_iota(jnp.int32, (16, area.shape[1]), 0)
+    stacked = jnp.zeros(row.shape, F32)
+    for i, value in enumerate((area * openness_ref[...], area, area * area)):
+        for part, rest in enumerate(parts_of(value)):
+            stacked = jnp.where(row == 4 * part + i, rest, stacked)
+    partial = lax.dot_general(
+        stacked.astype(BF16), member[...], (((1,), (1,)), ((), ())), preferred_element_type=F32
+    )
+    stat_low[low, 0:4] = partial[0:4] + partial[4:8] + partial[8:12]
+    stat_low[low, 4:8] = jnp.zeros((4, LANES), F32)
+
     lane = lax.broadcasted_iota(jnp.int32, (ROWS, LANES), 1).astype(F32)
 
     def build(d):
@@ -207,6 +229,9 @@
             total = total + buffer[m]
         return total
 
+    stat_low_copies = spread(stat_low, low, low_send.at[0], low_recv.at[0], low_of)
+    for d in range(1, YS):
+        pl.semaphore_signal(y_ready, inc=1, device_id=y_of(d), device_id_type=MESH)
     bins_copies = []
     for d in range(1, hours):
         copy = remote(bins.at[0], bins.at[d], hour_send.at[0, d], hour_recv.at[0, d], hour_of(d))
@@ -225,31 +250,6 @@
         copy.start()
         target_copies.append(copy)
 
-    for copy in small[3:]:
-        copy.wait()
-    area = area_ref[...]
-    zone_row = lax.broadcasted_iota(jnp.int32, member.shape, 0)
-    member[...] = jnp.where(zone_row == zone_ref[...], 1.0, 0.0).astype(BF16)
-
-    def parts_of(value):
-        first = value.astype(BF16).astype(F32)
-        second = (value - first).astype(BF16).astype(F32)
-        return first, second, value - first - second
-
-    row = lax.broadcasted_iota(jnp.int32, (16, area.shape[1]), 0)
-    stacked = jnp.zeros(row.shape, F32)
-    for i, value in enumerate((area * openness_ref[...], area, area * area)):
-        for part, rest in enumerate(parts_of(value)):
-            stacked = jnp.where(row == 4 * part + i, rest, stacked)
-    partial = lax.dot_general(
-        stacked.astype(BF16), member[...], (((1,), (1,)), ((), ())), preferred_element_type=F32
-    )
-    stat_low[low, 0:4] = partial[0:4] + partial[4:8] + partial[8:12]
-    stat_low[low, 4:8] = jnp.zeros((4, LANES), F32)
-
-    stat_low_copies = spread(stat_low, low, low_send.at[0], low_recv.at[0], low_of)
-    for d in range(1, YS):
-        pl.semaphore_signal(y_ready, inc=1, device_id=y_of(d), device_id_type=MESH)
     def sun_of(d):
         here = slice(d * block, (d + 1) * block)
         cross[d] = jnp.dot(weights[here, 0:whole], coef[0:whole, :], preferred_element_type=F32) + jnp.dot(
@@ -319,10 +319,26 @@
     shares = sums[0:1] / den
     share = jnp.sum(jnp.where(zone_lane == s, shares, 0.0), axis=1, keepdims=True)
 
+    lit_copies = []
+
+    def send_lit(d, first, last, kind):
+        rows = slice(first, last)
+        copy = remote(
+            lit_out.at[d, rows],
+            lit_hbm.at[rows, own_columns],
+            hour_send.at[kind, d],
+            hour_recv.at[kind, d],
+            hour_of(hours - d),
+        )
+        copy.start()
+        lit_copies.append(copy)
+
     for d in range(hours):
         level = lit[d] + share * cross[d]
         lit[d] = level
         lit_out[d] = level.astype(BF16)
+        if d:
+            send_lit(d, 0, 16, 3)
     own_out = pltpu.make_async_copy(lit_out.at[0], lit_hbm.at[:, own_columns], local_sem.at[0])
     own_out.start()
 
@@ -335,13 +351,11 @@
     local_grad = jnp.sum(terms, axis=1, keepdims=True)
     grad_column[in_column] = jnp.where(zone_lane == s, local_grad, 0.0)
     column_copies = spread(grad_column, in_column, column_send, column_recv, column_of)
-    lit_copies = []
-    for d in range(1, hours):
-        held = lit_hbm.at[:, own_columns]
-        copy = remote(lit_out.at[d], held, hour_send.at[3, d], hour_recv.at[3, d], hour_of(hours - d))
-        copy.start()
-        lit_copies.append(copy)
-    arrive(column_copies)
+    for d in (1,):
+        column_copies[d - 1].wait_recv()
+    for d in range(1, hours):
+        send_lit(d, 16, block, 4)
+    arrive([column_copies[d - 1] for d in range(1, 2 * hours * CORES) if d not in (1,)])
     grad_all[chip] = total_of(grad_column)
     across_copies = spread(grad_all, chip, across_send, across_recv, across_of)
     arrive(across_copies)
@@ -428,8 +442,8 @@
                 pltpu.VMEM((2 * hours * CORES, 1, LANES), F32),
                 pltpu.VMEM((PLANE // CORES, 1, LANES), F32),
                 pltpu.SemaphoreType.DMA((16,)),
-                pltpu.SemaphoreType.DMA((4, hours)),
-                pltpu.SemaphoreType.DMA((4, hours)),
+                pltpu.SemaphoreType.DMA((5, hours)),
+                pltpu.SemaphoreType.DMA((5, hours)),
                 pltpu.SemaphoreType.DMA((2, SIDE)),
                 pltpu.SemaphoreType.DMA((2, SIDE)),
                 pltpu.SemaphoreType.DMA((YS,)),

time: 37.7 us -> 36.3 us (0.963)
  Pallas kernels: 37 us -> 35.5 us
    pallas_call x1, Pallas kernels: 36.1 us -> 34.7 us  [step(): pl.pallas_call(functools.partial(kernel, hours, windows * sens), out_shap...]
where the time goes in v5:
time: 36.3 us; the launch traced here: 36.2 us
  Pallas kernels  35.5 us (98%)
  between operations  0.64 us (2%)
    pallas_call x1, Pallas kernels, step(): pl.pallas_call(functools.partial(kernel, hours, windows * sens), out_shap...  34.7 us
    pallas_call x1, Pallas kernels, step(): pl.pallas_call(hand_over, out_shape=(jax.ShapeDtypeStruct(lit.shape, BF16...  0.81 us

profile of v5, /device:TPU:1, one launch (start us, length us, event | category | flops | bytes accessed | tf_op | source)
XLA Modules:
  0.0 36.2 jit_solution(17549573641151486885)
XLA Ops:
  0.6 34.7 %shard_map.113 = (bf16[128,2048]{1,0:T(8,128)(2,1)S(1)}, f32[1,1024]{1,0:T(1,128)S(1)}) custom-call(bf16[146,128]{1,0:T(8,128)(2,1)} %bitcast.7, bf16[146,2048]{1,0:T(8,128)(2,1)} %open_hbm.1, bf16[146,2048]{1,0:T(8,128)(2,1)} %closed_hbm.1, bf16[5165,512]{1,0:T(8,128)(2,1)} %coef_hbm.1, s32[4,128]{1,0:T(4,128)} %bitcast.11, bf16[4,128]{1,0:T(4,128)(2,1)} %bitcast.12, ...), custom_call_target="tpu_custom_call" | custom-call | tf_op jit(solution)/shard_map/pallas_call | solution.py:411
  35.3 0.8 %shard_map.114 = (bf16[128,2048]{1,0:T(8,128)(2,1)}, f32[1,1024]{1,0:T(1,128)}) custom-call(bf16[128,2048]{1,0:T(8,128)(2,1)S(1)} %get-tuple-element.6.lit_in, f32[1,1024]{1,0:T(1,128)S(1)} %get-tuple-element.7.new_in), custom_call_target="tpu_custom_call" | custom-call | tf_op jit(solution)/shard_map/pallas_call | solution.py:479
